TPU v7x, 32 devices: a whole 2x2x4 slice. The times are simulated.
32 devices in a mesh: league: 4 (over x, core), env: 8 (over z, y).
Axes of the slice: x: 2, y: 2, z: 4, core: 2. Of those that a mesh axis runs over, the one named last changes fastest.
Arguments:
- obs_own: bfloat16 [4, 2, 128, 16, 2048], P('league', None, 'env'), may hold values from -6 to 6
- obs_opp: bfloat16 [4, 2, 128, 16, 2048], P('league', None, 'env'), may hold values from -6 to 6
- actions: int32 [4, 2, 2, 128, 16], P('league', None, None, 'env'), may hold values from 0 to 255
- opponent_picks: int32 [4, 2], P('league'), may hold values from 0 to 3
- policy_weight: bfloat16 [4, 2048, 2048], P('league', 'env'), may hold values from -0.125 to 0.125
- policy_gain: bfloat16 [4, 2048], P('league'), may hold values from 0.25 to 1.75
- action_table: bfloat16 [256, 2048], replicated, may hold values from -6 to 6
- value_gain: bfloat16 [2048], replicated, may hold values from 0.25 to 1.75
- value_up: bfloat16 [2048, 1024], replicated, may hold values from -0.125 to 0.125
- value_out: bfloat16 [1024], replicated, may hold values from -0.1875 to 0.1875
Outputs:
- learner_rows: bfloat16 [4, 2, 16, 2048, 128], P('league', None, None, 'env')
- values: float32 [4, 2, 128, 16], P('league', None, 'env')
All inputs are finite; a program needn't handle non-finite values.
Results may differ from a plain program's by a relative error of at most 0.0054.
Values may be sent and summed in bfloat16 or wider, within the bound.
A program may use at most 128 MiB of HBM per device.

v0:
```python
import jax
import jax.numpy as jnp
from jax import lax
from jax.sharding import PartitionSpec as P


def rms_norm(inputs, gain):
    scale = lax.rsqrt(jnp.mean(inputs * inputs, axis=-1, keepdims=True) + 1e-05)
    return inputs * scale * gain.astype(jnp.float32)


def local(
    obs_own,
    obs_opp,
    actions,
    opponent_picks,
    policy_weight,
    policy_gain,
    action_table,
    value_gain,
    value_up,
    value_out,
):
    round_count = obs_own.shape[1]
    env_count = obs_own.shape[2]
    step_count = obs_own.shape[3]
    model_width = obs_own.shape[4]
    row_count = env_count * step_count
    weight_shard = policy_weight[0]
    own_gain = policy_gain[0]
    group_count = lax.axis_size("league")
    my_group = lax.axis_index("league")
    own_inputs = obs_own[0].reshape(round_count * row_count, model_width).astype(jnp.float32)
    own_normed = rms_norm(own_inputs, own_gain).astype(jnp.bfloat16)
    own_whole = lax.all_gather(weight_shard, "env", axis=0, tiled=True)
    own_state = own_inputs + jnp.dot(own_normed, own_whole, preferred_element_type=jnp.float32)
    every_pick = lax.all_gather(opponent_picks, "league", axis=0, tiled=True)
    action_range = jnp.arange(action_table.shape[0], dtype=jnp.int32)
    traj_list = []
    value_list = []
    for round_index in range(round_count):
        opp_raw = obs_opp[0, round_index].reshape(row_count, model_width)
        opp_inputs = opp_raw.astype(jnp.float32)
        all_rows = lax.all_gather(opp_raw, "league", axis=0, tiled=True)
        all_normed = rms_norm(all_rows.astype(jnp.float32), own_gain).astype(jnp.bfloat16)
        products = jnp.dot(all_normed, own_whole, preferred_element_type=jnp.float32)
        served = (every_pick[:, round_index] == my_group).astype(jnp.float32)
        products = (
            products.reshape(group_count, row_count, model_width) * served[:, None, None]
        ).reshape(group_count * row_count, model_width)
        opp_state = opp_inputs + lax.psum_scatter(
            products, "league", scatter_dimension=0, tiled=True
        )
        own_ids = actions[0, 0, round_index].reshape(row_count)
        opp_ids = actions[0, 1, round_index].reshape(row_count)
        onehot = (own_ids[:, None] == action_range[None, :]).astype(jnp.bfloat16) + (
            opp_ids[:, None] == action_range[None, :]
        ).astype(jnp.bfloat16)
        action_sum = jnp.dot(onehot, action_table, preferred_element_type=jnp.float32)
        round_state = lax.dynamic_slice_in_dim(own_state, round_index * row_count, row_count, 0)
        joint_sum = round_state + opp_state + action_sum
        joint_row = rms_norm(joint_sum, value_gain).astype(jnp.bfloat16)
        value_hidden = jax.nn.silu(
            jnp.dot(joint_row, value_up, preferred_element_type=jnp.float32)
        ).astype(jnp.bfloat16)
        value_est = jnp.dot(value_hidden, value_out, preferred_element_type=jnp.float32)
        value_list.append(value_est.reshape(env_count, step_count))
        time_block = joint_row.reshape(env_count, step_count, model_width).transpose(1, 2, 0)
        traj_list.append(lax.all_to_all(time_block, "env", split_axis=1, concat_axis=2, tiled=True))
    learner_rows = jnp.stack(traj_list)
    values = jnp.stack(value_list)
    return (learner_rows[None], values[None])


def solution(mesh):
    in_specs = (
        P("league", None, "env", None, None),
        P("league", None, "env", None, None),
        P("league", None, None, "env", None),
        P("league", None),
        P("league", "env", None),
        P("league", None),
        P(),
        P(),
        P(),
        P(),
    )
    out_specs = (P("league", None, None, "env", None), P("league", None, "env", None))
    return jax.shard_map(local, mesh=mesh, in_specs=in_specs, out_specs=out_specs, check_vma=False)
```

profile of v0, /device:TPU:12, one launch (start us, length us, event | category | flops | bytes accessed | tf_op | source)
XLA Modules:
  0.0 479.5 jit_solution(18280044370628031255)
XLA Ops:
  7.2 3.2 fusion.49
  12.0 5.0 %all-gather.1 = s32[4,1,2]{2,1,0:T(1,128)S(1)} all-gather(s32[1,1,2]{2,1,0:T(1,128)S(1)} %bitcast.98), channel_id=1, replica_groups=mesh['league'=4,'env'=8] {'league'}, dimensions={0}, use_global_device_ids=true | all-gather | bytes 40 | tf_op jit(solution)/shard_map/all_gather | solution.py:37
  17.3 29.0 %all-gather.6.cloned.1.call-done = bf16[1024,2048]{1,0:T(8,128)(2,1)} async-done(((bf16[256,2048]{1,0:T(8,128)(2,1)}), bf16[1024,2048]{1,0:T(8,128)(2,1)}) %all-gather.6.cloned.1.call-update) | async-done | bytes 4194320 | tf_op jit(solution)/shard_map/all_gather | solution.py:44
  46.2 3.1 fusion
  49.3 121.2 %all-gather.10.cloned.1.call-done = bf16[1,2048,2048]{2,1,0:T(8,128)(2,1)} async-done(((bf16[1,256,2048]{2,1,0:T(8,128)(2,1)}), bf16[1,2048,2048]{2,1,0:T(8,128)(2,1)}) %all-gather.10.cloned.1.call-update) | async-done | bytes 8388624 | tf_op jit(solution)/shard_map/all_gather | solution.py:35
  170.5 14.5 %fusion.12 = f32[1024,2048]{1,0:T(8,128)} fusion(bf16[1,2048,2048]{2,1,0:T(8,128)(2,1)} %all-gather.10.cloned.1.call-done, bf16[1024,2048]{1,0:T(8,128)(2,1)} %all-gather.6.cloned.1.call-done, f32[1024]{0:T(1024)S(1)} %bitcast.94, f32[2048]{0:T(1024)S(1)} %bitcast.90, f32[1024]{0:T(1024)S(1)} %add_rsqrt_fusion.2), kind=kOutput, calls=%fused_computation.16 | convolution fusion | flops 8600420352 | bytes 20987904 | tf_op jit(solution)/shard_map/dot_general | solution.py:46
  185.3 22.3 %all-gather.8.cloned.1.call-done = bf16[1024,2048]{1,0:T(8,128)(2,1)} async-done(((bf16[256,2048]{1,0:T(8,128)(2,1)}), bf16[1024,2048]{1,0:T(8,128)(2,1)}) %all-gather.8.cloned.1.call-update) | async-done | bytes 4194320 | tf_op jit(solution)/shard_map/all_gather | solution.py:44
  207.6 3.2 fusion.3
  211.0 13.6 %fusion.15 = f32[1024,2048]{1,0:T(8,128)} fusion(bf16[1,2048,2048]{2,1,0:T(8,128)(2,1)} %all-gather.10.cloned.1.call-done, bf16[1024,2048]{1,0:T(8,128)(2,1)S(1)} %copy-done.6, f32[1024]{0:T(1024)S(1)} %bitcast.95, f32[1024]{0:T(1024)S(1)} %add_rsqrt_fusion.1, f32[2048]{0:T(1024)S(1)} %bitcast.91), kind=kOutput, calls=%fused_computation.17 | convolution fusion | flops 8600420352 | bytes 20987904 | tf_op jit(solution)/shard_map/dot_general | solution.py:46
  225.6 0.8 copy-done.4
  227.7 1.0 copy-done.5
  228.7 9.6 %bitcast_add_fusion = f32[512,2048]{1,0:T(8,128)} fusion(bf16[1,2,16,16,2048]{4,3,2,1,0:T(8,128)(2,1)S(1)} %copy-done.5, bf16[512,2048]{1,0:T(8,128)(2,1)S(1)} %fusion.22, bf16[1,2048,2048]{2,1,0:T(8,128)(2,1)} %all-gather.10.cloned.1.call-done), kind=kOutput, calls=%fused_computation.18 | convolution fusion | flops 4297064448 | bytes 16777216 | tf_op jit(solution)/shard_map/dot_general | solution.py:36
  238.4 43.4 %reduce-scatter.3.cloned.1.call-done = f32[256,2048]{1,0:T(8,128)} async-done(((f32[1024,2048]{1,0:T(8,128)}), f32[256,2048]{1,0:T(8,128)}) %reduce-scatter.3.cloned.1.call-update) | async-done | bytes 2097168 | tf_op jit(solution)/shard_map/reduce_scatter | solution.py:51
  281.8 4.2 multiply_reduce_fusion.1
  286.0 70.2 %reduce-scatter.5.cloned.1.call-done = f32[256,2048]{1,0:T(8,128)} async-done(((f32[1024,2048]{1,0:T(8,128)}), f32[256,2048]{1,0:T(8,128)}) %reduce-scatter.5.cloned.1.call-update) | async-done | bytes 2097168 | tf_op jit(solution)/shard_map/reduce_scatter | solution.py:51
  356.1 3.1 multiply_reduce_fusion
  359.7 8.8 %copy.27 = bf16[16,16,2048]{0,1,2:T(8,128)(2,1)} copy(bf16[16,16,2048]{2,1,0:T(8,128)(2,1)S(1)} %bitcast.87) | data formatting | bytes 2097152 | tf_op jit(solution)/shard_map/reshape | solution.py:68
  368.5 7.5 %bitcast_bitcast_fusion = bf16[2048,16,16]{2,1,0:T(8,128)(2,1)} fusion(bf16[16,16,2048]{0,1,2:T(8,128)(2,1)} %copy.27), kind=kLoop, calls=%fused_computation.71 | loop fusion | bytes 2097152
  376.0 11.2 %reshape.107 = bf16[8,2,32768]{2,1,0:T(2,128)(2,1)} reshape(bf16[2048,16,16]{2,1,0:T(8,128)(2,1)} %bitcast_bitcast_fusion) | data formatting | bytes 2097152
  387.2 6.0 %all-to-all-start.1 = ((bf16[8,2,32768]{2,1,0:T(2,128)(2,1)}), bf16[8,2,32768]{2,1,0:T(2,128)(2,1)S(1)}, u32[]{:S(2)}, u32[]{:S(2)}) async-start(bf16[8,2,32768]{2,1,0:T(2,128)(2,1)} %reshape.107), calls=%async_computation.3 | async-start | bytes 2097152 | tf_op jit(solution)/shard_map/all_to_all | solution.py:69
  393.3 8.8 %copy.24 = bf16[16,16,2048]{0,1,2:T(8,128)(2,1)} copy(bf16[16,16,2048]{2,1,0:T(8,128)(2,1)S(1)} %bitcast.86) | data formatting | bytes 2097152 | tf_op jit(solution)/shard_map/reshape | solution.py:68
  402.1 7.5 %bitcast_bitcast_fusion.1 = bf16[2048,16,16]{2,1,0:T(8,128)(2,1)} fusion(bf16[16,16,2048]{0,1,2:T(8,128)(2,1)} %copy.24), kind=kLoop, calls=%fused_computation.72 | loop fusion | bytes 2097152
  409.5 11.2 %reshape.109 = bf16[8,2,32768]{2,1,0:T(2,128)(2,1)} reshape(bf16[2048,16,16]{2,1,0:T(8,128)(2,1)} %bitcast_bitcast_fusion.1) | data formatting | bytes 2097152
  420.8 6.0 %all-to-all-start = ((bf16[8,2,32768]{2,1,0:T(2,128)(2,1)}), bf16[8,2,32768]{2,1,0:T(2,128)(2,1)S(1)}, u32[]{:S(2)}, u32[]{:S(2)}) async-start(bf16[8,2,32768]{2,1,0:T(2,128)(2,1)} %reshape.109), calls=%async_computation.1 | async-start | bytes 2097152 | tf_op jit(solution)/shard_map/all_to_all | solution.py:69
  426.8 3.9 fusion.30
  430.8 4.0 fusion.29
  435.5 7.5 %reshape.108 = bf16[2048,16,16]{2,1,0:T(8,128)(2,1)} reshape(bf16[8,2,32768]{2,1,0:T(2,128)(2,1)S(1)} %all-to-all-done.1) | data formatting | bytes 2097152
  443.1 9.1 %copy.29 = bf16[16,256,8,16]{1,3,2,0:T(8,128)(2,1)} copy(bf16[16,256,8,16]{3,0,1,2:T(8,128)(2,1)} %bitcast.80) | data formatting | bytes 2097152 | tf_op jit(solution)/shard_map/all_to_all | solution.py:69
  452.2 7.5 %reshape.110 = bf16[2048,16,16]{2,1,0:T(8,128)(2,1)} reshape(bf16[8,2,32768]{2,1,0:T(2,128)(2,1)S(1)} %all-to-all-done) | data formatting | bytes 2097152
  459.7 9.1 %copy.26 = bf16[16,256,8,16]{1,3,2,0:T(8,128)(2,1)} copy(bf16[16,256,8,16]{3,0,1,2:T(8,128)(2,1)} %bitcast.81) | data formatting | bytes 2097152 | tf_op jit(solution)/shard_map/all_to_all | solution.py:69
  468.8 1.7 maximum_bitcast_fusion
  470.6 2.4 copy.30
  (63 shorter events, 5.7 us)
Async XLA Ops:
  7.2 274.6 %copy-start = (bf16[256,2048]{1,0:T(8,128)(2,1)S(1)}, bf16[256,2048]{1,0:T(8,128)(2,1)}, u32[]{:S(2)}) copy-start(bf16[256,2048]{1,0:T(8,128)(2,1)} %param.16) | copy-start | bytes 3145732
  7.2 4.8 %copy-start.13 = (s32[1,2]{1,0:T(1,128)S(1)}, s32[1,2]{1,0:T(1,128)}, u32[]{:S(2)}) copy-start(s32[1,2]{1,0:T(1,128)} %param.13) | copy-start | bytes 28
  7.2 10.1 %copy-start.10 = (bf16[1,2048]{1,0:T(2,128)(2,1)S(1)}, bf16[1,2048]{1,0:T(2,128)(2,1)}, u32[]{:S(2)}) copy-start(bf16[1,2048]{1,0:T(2,128)(2,1)} %param.15) | copy-start | bytes 12292
  7.2 39.0 %all-gather.6.cloned.1.call-start = ((), (), s32[]{:S(2)}) async-start(), calls=%async_computation.4 | async-start | bytes 5242880 | tf_op jit(solution)/shard_map/all_gather | solution.py:44
  10.5 160.0 %all-gather.10.cloned.1.call-start = ((), (), s32[]{:S(2)}) async-start(), calls=%async_computation.8 | async-start | bytes 9437184 | tf_op jit(solution)/shard_map/all_gather | solution.py:35
  11.2 196.4 %all-gather.8.cloned.1.call-start = ((), (), s32[]{:S(2)}) async-start(), calls=%async_computation.6 | async-start | bytes 5242880 | tf_op jit(solution)/shard_map/all_gather | solution.py:44
  12.0 269.8 %reduce-scatter.3.cloned.1.call-start = ((), (), s32[]{:S(2)}) async-start(), calls=%async_computation.5 | async-start | bytes 10485760 | tf_op jit(solution)/shard_map/reduce_scatter | solution.py:51
  185.0 171.1 %reduce-scatter.5.cloned.1.call-start = ((), (), s32[]{:S(2)}) async-start(), calls=%async_computation.7 | async-start | bytes 10485760 | tf_op jit(solution)/shard_map/reduce_scatter | solution.py:51
  207.6 3.4 copy-start.6
  224.6 0.8 copy-start.9
  224.6 1.7 copy-start.4
  224.6 2.3 copy-start.11
  227.1 1.6 copy-start.5
  228.7 53.0 %copy-start.2 = (bf16[1,1,16,16,2048]{4,3,2,1,0:T(8,128)(2,1)S(1)}, bf16[1,1,16,16,2048]{4,3,2,1,0:T(8,128)(2,1)}, u32[]{:S(2)}) copy-start(bf16[1,1,16,16,2048]{4,3,2,1,0:T(8,128)(2,1)} %get-tuple-element.8) | copy-start | bytes 3145732
  238.4 117.8 %copy-start.1 = (bf16[1,1,16,16,2048]{4,3,2,1,0:T(8,128)(2,1)S(1)}, bf16[1,1,16,16,2048]{4,3,2,1,0:T(8,128)(2,1)}, u32[]{:S(2)}) copy-start(bf16[1,1,16,16,2048]{4,3,2,1,0:T(8,128)(2,1)} %get-tuple-element.9) | copy-start | bytes 3145732
  356.1 3.1 copy-start.3
  359.7 8.8 %copy-start.8 = (bf16[256,2048]{1,0:T(8,128)(2,1)}, bf16[256,2048]{1,0:T(8,128)(2,1)S(1)}, u32[]{:S(2)}) copy-start(bf16[256,2048]{1,0:T(8,128)(2,1)S(1)} %get-tuple-element.15) | copy-start | bytes 3145732
  359.7 33.6 %copy-start.7 = (bf16[256,2048]{1,0:T(8,128)(2,1)}, bf16[256,2048]{1,0:T(8,128)(2,1)S(1)}, u32[]{:S(2)}) copy-start(bf16[256,2048]{1,0:T(8,128)(2,1)S(1)} %get-tuple-element.14) | copy-start | bytes 3145732
  387.2 33.5 %all-to-all-start.1 = ((bf16[8,2,32768]{2,1,0:T(2,128)(2,1)}), bf16[8,2,32768]{2,1,0:T(2,128)(2,1)S(1)}, u32[]{:S(2)}, u32[]{:S(2)}) async-start(bf16[8,2,32768]{2,1,0:T(2,128)(2,1)} %reshape.107), calls=%async_computation.3 | async-start | bytes 2097152 | tf_op jit(solution)/shard_map/all_to_all | solution.py:69
  409.5 17.2 %copy-start.12 = (bf16[1024]{0:T(1024)(128)(2,1)S(1)}, bf16[1024]{0:T(1024)(128)(2,1)}, u32[]{:S(2)}) copy-start(bf16[1024]{0:T(1024)(128)(2,1)} %param.19) | copy-start | bytes 6148
  420.8 31.4 %all-to-all-start = ((bf16[8,2,32768]{2,1,0:T(2,128)(2,1)}), bf16[8,2,32768]{2,1,0:T(2,128)(2,1)S(1)}, u32[]{:S(2)}, u32[]{:S(2)}) async-start(bf16[8,2,32768]{2,1,0:T(2,128)(2,1)} %reshape.109), calls=%async_computation.1 | async-start | bytes 2097152 | tf_op jit(solution)/shard_map/all_to_all | solution.py:69
Sparse Core Ops, SparseCore 0:
  10.6 35.5 all-gather.5
  48.3 122.0 all-gather.9
  172.0 35.4 all-gather.7
  210.0 71.7 reduce-scatter.2
  284.4 71.7 reduce-scatter.4
where the time goes:
time: 482 us; the launch traced here: 479 us
  waiting for transfers between devices  287 us (60%)
  local copies, waits for them, and re-layouts  97.5 us (20%)
  matrix products  53 us (11%)
  between operations  13.9 us (3%)
  starting transfers between devices  12.4 us (3%)
  other arithmetic  10.2 us (2%)
  blocking collectives  5.04 us (1%)
    all_gather x1, waiting for transfers between devices, local(): own_whole = lax.all_gather(weight_shard, 'env', axis=0, tiled=True)  121 us
    reduce_scatter x2, waiting for transfers between devices, local(): lax.psum_scatter(products, 'league', scatter_dimension=0, tiled=True)  114 us
    unnamed x39, local copies, waits for them, and re-layouts  57.8 us
    all_gather x2, waiting for transfers between devices, local(): all_rows = lax.all_gather(opp_raw, 'league', axis=0, tiled=True)  51.3 us
    dot_general x2, matrix products, local(): jnp.dot(all_normed, own_whole, preferred_element_type=jnp.float32)  28.1 us
    all_to_all x2, local copies, waits for them, and re-layouts, local(): lax.all_to_all(time_block, 'env', split_axis=1, concat_axis=2, tiled=True)  18.2 us
    reshape x2, local copies, waits for them, and re-layouts, local(): joint_row.reshape(env_count, step_count, model_width).transpose(1, 2, 0)  17.6 us
    all_to_all x2, starting transfers between devices, local(): lax.all_to_all(time_block, 'env', split_axis=1, concat_axis=2, tiled=True)  12 us
  transfers between devices with their start and end apart: 7, of which 5 were waited for; matrix products, arithmetic and copies ran while one was open for 21% of the time, Pallas kernels for 0%

commit v1 on v0

--- a/solution.py
+++ b/solution.py
@@ -47,10 +47,9 @@
         served = (every_pick[:, round_index] == my_group).astype(jnp.float32)
         products = (
             products.reshape(group_count, row_count, model_width) * served[:, None, None]
-        ).reshape(group_count * row_count, model_width)
-        opp_state = opp_inputs + lax.psum_scatter(
-            products, "league", scatter_dimension=0, tiled=True
-        )
+        ).astype(jnp.bfloat16)
+        answers = lax.all_to_all(products, "league", split_axis=0, concat_axis=0, tiled=True)
+        opp_state = opp_inputs + jnp.sum(answers.astype(jnp.float32), axis=0)
         own_ids = actions[0, 0, round_index].reshape(row_count)
         opp_ids = actions[0, 1, round_index].reshape(row_count)
         onehot = (own_ids[:, None] == action_range[None, :]).astype(jnp.bfloat16) + (

time: 482 us -> 432 us (0.90)
  waiting for transfers between devices: 287 us -> 226 us
  other arithmetic: 10.2 us -> 24.9 us
  matrix products: 53 us -> 41.7 us
  starting transfers between devices: 12.4 us -> 22.1 us
    reduce_scatter x2 -> x0, waiting for transfers between devices: 114 us -> none  [local(): lax.psum_scatter(products, 'league', scatter_dimension=0, tiled=True)]
    all_to_all x0 -> x2, waiting for transfers between devices: none -> 46.4 us  [local(): lax.all_to_all(products, 'league', split_axis=0, concat_axis=0, tiled=True)]
    all_to_all x0 -> x2, starting transfers between devices: none -> 9.95 us  [local(): lax.all_to_all(products, 'league', split_axis=0, concat_axis=0, tiled=True)]
    reduce_sum x0 -> x2, other arithmetic: none -> 8.25 us  [local(): opp_state = opp_inputs + jnp.sum(answers.astype(jnp.float32), axis=0)]
    convert_element_type x0 -> x2, other arithmetic: none -> 6.41 us  [local(): products = (products.reshape(group_count, row_count, model_width) * serve...]
    all_gather x2, waiting for transfers between devices: 51.3 us -> 57.1 us  [local(): all_rows = lax.all_gather(opp_raw, 'league', axis=0, tiled=True)]
    unnamed x39 -> x38, local copies, waits for them, and re-layouts: 57.8 us -> 56 us
  transfers between devices with their start and end apart: 7 -> 7, of which waited for: 5 -> 5; matrix products, arithmetic and copies ran while one was open for 21% -> 24% of each run, Pallas kernels for 0% -> 0%
where the time goes in v1:
time: 432 us; the launch traced here: 429 us
  waiting for transfers between devices  226 us (52%)
  local copies, waits for them, and re-layouts  95.6 us (22%)
  matrix products  41.7 us (10%)
  other arithmetic  24.9 us (6%)
  starting transfers between devices  22.1 us (5%)
  between operations  14 us (3%)
  blocking collectives  5.04 us (1%)
    all_gather x1, waiting for transfers between devices, local(): own_whole = lax.all_gather(weight_shard, 'env', axis=0, tiled=True)  121 us
    all_gather x2, waiting for transfers between devices, local(): all_rows = lax.all_gather(opp_raw, 'league', axis=0, tiled=True)  57.1 us
    unnamed x38, local copies, waits for them, and re-layouts  56 us
    all_to_all x2, waiting for transfers between devices, local(): lax.all_to_all(products, 'league', split_axis=0, concat_axis=0, tiled=True)  46.4 us
    dot_general x2, matrix products, local(): jnp.dot(all_normed, own_whole, preferred_element_type=jnp.float32)  23.9 us
    all_to_all x2, local copies, waits for them, and re-layouts, local(): lax.all_to_all(time_block, 'env', split_axis=1, concat_axis=2, tiled=True)  18.2 us
    reshape x2, local copies, waits for them, and re-layouts, local(): joint_row.reshape(env_count, step_count, model_width).transpose(1, 2, 0)  17.6 us
    all_to_all x2, starting transfers between devices, local(): lax.all_to_all(time_block, 'env', split_axis=1, concat_axis=2, tiled=True)  12 us
  transfers between devices with their start and end apart: 7, of which 5 were waited for; matrix products, arithmetic and copies ran while one was open for 24% of the time, Pallas kernels for 0%

profile of v1, /device:TPU:12, one launch (start us, length us, event | category | flops | bytes accessed | tf_op | source)
XLA Modules:
  0.0 429.4 jit_solution(11888221236370943280)
XLA Ops:
  7.2 3.2 fusion.43
  12.0 5.0 %all-gather.1 = s32[4,1,2]{2,1,0:T(1,128)S(1)} all-gather(s32[1,1,2]{2,1,0:T(1,128)S(1)} %bitcast.90), channel_id=1, replica_groups=mesh['league'=4,'env'=8] {'league'}, dimensions={0}, use_global_device_ids=true | all-gather | bytes 40 | tf_op jit(solution)/shard_map/all_gather | solution.py:37
  17.1 29.1 %all-gather.6.cloned.1.call-done = bf16[1024,2048]{1,0:T(8,128)(2,1)} async-done(((bf16[256,2048]{1,0:T(8,128)(2,1)}), bf16[1024,2048]{1,0:T(8,128)(2,1)}) %all-gather.6.cloned.1.call-update) | async-done | bytes 4194320 | tf_op jit(solution)/shard_map/all_gather | solution.py:44
  46.2 3.1 fusion
  49.3 121.2 %all-gather.10.cloned.1.call-done = bf16[1,2048,2048]{2,1,0:T(8,128)(2,1)} async-done(((bf16[1,256,2048]{2,1,0:T(8,128)(2,1)}), bf16[1,2048,2048]{2,1,0:T(8,128)(2,1)}) %all-gather.10.cloned.1.call-update) | async-done | bytes 8388624 | tf_op jit(solution)/shard_map/all_gather | solution.py:35
  170.5 12.6 %fusion.8 = f32[1024,2048]{1,0:T(8,128)S(1)} fusion(bf16[1,2048,2048]{2,1,0:T(8,128)(2,1)} %all-gather.10.cloned.1.call-done, bf16[1024,2048]{1,0:T(8,128)(2,1)} %all-gather.6.cloned.1.call-done, f32[2048]{0:T(1024)S(1)} %bitcast.84, f32[1024]{0:T(1024)S(1)} %add_rsqrt_fusion.2), kind=kOutput, calls=%fused_computation.12 | convolution fusion | flops 8598323200 | bytes 20983808 | tf_op jit(solution)/shard_map/dot_general | solution.py:46
  183.0 3.2 multiply_convert_fusion.1
  186.3 4.9 %all-to-all-start = ((bf16[4,256,2048]{2,1,0:T(8,128)(2,1)}), bf16[4,256,2048]{2,1,0:T(8,128)(2,1)}, u32[]{:S(2)}, u32[]{:S(2)}) async-start(bf16[4,256,2048]{2,1,0:T(8,128)(2,1)} %multiply_convert_fusion.1), calls=%async_computation | async-start | bytes 8388608 | tf_op jit(solution)/shard_map/all_to_all | solution.py:51
  191.2 28.1 %all-gather.8.cloned.1.call-done = bf16[1024,2048]{1,0:T(8,128)(2,1)} async-done(((bf16[256,2048]{1,0:T(8,128)(2,1)}), bf16[1024,2048]{1,0:T(8,128)(2,1)}) %all-gather.8.cloned.1.call-update) | async-done | bytes 4194320 | tf_op jit(solution)/shard_map/all_gather | solution.py:44
  219.2 3.2 fusion.3
  222.7 11.3 %fusion.6 = f32[1024,2048]{1,0:T(8,128)S(1)} fusion(bf16[1,2048,2048]{2,1,0:T(8,128)(2,1)} %all-gather.10.cloned.1.call-done, bf16[1024,2048]{1,0:T(8,128)(2,1)S(1)} %copy-done.7, f32[1024]{0:T(1024)S(1)} %add_rsqrt_fusion.1, f32[2048]{0:T(1024)S(1)} %bitcast.85), kind=kOutput, calls=%fused_computation.10 | convolution fusion | flops 8598323200 | bytes 20983808 | tf_op jit(solution)/shard_map/dot_general | solution.py:46
  234.0 3.2 multiply_convert_fusion
  237.2 13.8 %all-to-all-done = bf16[4,256,2048]{2,1,0:T(8,128)(2,1)} async-done(((bf16[4,256,2048]{2,1,0:T(8,128)(2,1)}), bf16[4,256,2048]{2,1,0:T(8,128)(2,1)}, u32[]{:S(2)}, u32[]{:S(2)}) %all-to-all-start) | async-done | bytes 4194336 | tf_op jit(solution)/shard_map/all_to_all | solution.py:51
  251.0 5.0 %all-to-all-start.2 = ((bf16[4,256,2048]{2,1,0:T(8,128)(2,1)}), bf16[4,256,2048]{2,1,0:T(8,128)(2,1)}, u32[]{:S(2)}, u32[]{:S(2)}) async-start(bf16[4,256,2048]{2,1,0:T(8,128)(2,1)} %multiply_convert_fusion), calls=%async_computation.2 | async-start | bytes 8388608 | tf_op jit(solution)/shard_map/all_to_all | solution.py:51
  257.5 7.0 %bitcast_add_fusion = f32[512,2048]{1,0:T(8,128)S(1)} fusion(bf16[1,2,16,16,2048]{4,3,2,1,0:T(8,128)(2,1)S(1)} %copy-done.4, bf16[512,2048]{1,0:T(8,128)(2,1)S(1)} %fusion.16, bf16[1,2048,2048]{2,1,0:T(8,128)(2,1)} %all-gather.10.cloned.1.call-done), kind=kOutput, calls=%fused_computation.20 | convolution fusion | flops 4297064448 | bytes 16777216 | tf_op jit(solution)/shard_map/dot_general | solution.py:36
  264.5 4.8 %convert_reduce_fusion.1 = f32[256,2048]{1,0:T(8,128)S(1)} fusion(bf16[4,256,2048]{2,1,0:T(8,128)(2,1)} %all-to-all-done), kind=kLoop, calls=%fused_computation.18 | loop fusion | flops 3670016 | bytes 6291456 | tf_op jit(solution)/shard_map/reduce_sum | solution.py:52
  271.5 32.6 %all-to-all-done.2 = bf16[4,256,2048]{2,1,0:T(8,128)(2,1)} async-done(((bf16[4,256,2048]{2,1,0:T(8,128)(2,1)}), bf16[4,256,2048]{2,1,0:T(8,128)(2,1)}, u32[]{:S(2)}, u32[]{:S(2)}) %all-to-all-start.2) | async-done | bytes 4194336 | tf_op jit(solution)/shard_map/all_to_all | solution.py:51
  304.1 3.4 convert_reduce_fusion
  309.6 8.8 %copy.27 = bf16[16,16,2048]{0,1,2:T(8,128)(2,1)} copy(bf16[16,16,2048]{2,1,0:T(8,128)(2,1)S(1)} %bitcast.81) | data formatting | bytes 2097152 | tf_op jit(solution)/shard_map/reshape | solution.py:67
  318.4 7.5 %bitcast_bitcast_fusion = bf16[2048,16,16]{2,1,0:T(8,128)(2,1)} fusion(bf16[16,16,2048]{0,1,2:T(8,128)(2,1)} %copy.27), kind=kLoop, calls=%fused_computation.71 | loop fusion | bytes 2097152
  325.9 11.2 %reshape.109 = bf16[8,2,32768]{2,1,0:T(2,128)(2,1)} reshape(bf16[2048,16,16]{2,1,0:T(8,128)(2,1)} %bitcast_bitcast_fusion) | data formatting | bytes 2097152
  337.1 6.0 %all-to-all-start.3 = ((bf16[8,2,32768]{2,1,0:T(2,128)(2,1)}), bf16[8,2,32768]{2,1,0:T(2,128)(2,1)S(1)}, u32[]{:S(2)}, u32[]{:S(2)}) async-start(bf16[8,2,32768]{2,1,0:T(2,128)(2,1)} %reshape.109), calls=%async_computation.3 | async-start | bytes 2097152 | tf_op jit(solution)/shard_map/all_to_all | solution.py:68
  343.2 8.8 %copy.24 = bf16[16,16,2048]{0,1,2:T(8,128)(2,1)} copy(bf16[16,16,2048]{2,1,0:T(8,128)(2,1)S(1)} %bitcast.80) | data formatting | bytes 2097152 | tf_op jit(solution)/shard_map/reshape | solution.py:67
  352.0 7.5 %bitcast_bitcast_fusion.1 = bf16[2048,16,16]{2,1,0:T(8,128)(2,1)} fusion(bf16[16,16,2048]{0,1,2:T(8,128)(2,1)} %copy.24), kind=kLoop, calls=%fused_computation.72 | loop fusion | bytes 2097152
  359.5 11.2 %reshape.111 = bf16[8,2,32768]{2,1,0:T(2,128)(2,1)} reshape(bf16[2048,16,16]{2,1,0:T(8,128)(2,1)} %bitcast_bitcast_fusion.1) | data formatting | bytes 2097152
  370.7 6.0 %all-to-all-start.1 = ((bf16[8,2,32768]{2,1,0:T(2,128)(2,1)}), bf16[8,2,32768]{2,1,0:T(2,128)(2,1)S(1)}, u32[]{:S(2)}, u32[]{:S(2)}) async-start(bf16[8,2,32768]{2,1,0:T(2,128)(2,1)} %reshape.111), calls=%async_computation.1 | async-start | bytes 2097152 | tf_op jit(solution)/shard_map/all_to_all | solution.py:68
  376.7 3.9 fusion.24
  380.7 4.0 fusion.23
  385.5 7.6 %reshape.110 = bf16[2048,16,16]{2,1,0:T(8,128)(2,1)} reshape(bf16[8,2,32768]{2,1,0:T(2,128)(2,1)S(1)} %all-to-all-done.3) | data formatting | bytes 2097152
  393.0 9.1 %copy.29 = bf16[16,256,8,16]{1,3,2,0:T(8,128)(2,1)} copy(bf16[16,256,8,16]{3,0,1,2:T(8,128)(2,1)} %bitcast.72) | data formatting | bytes 2097152 | tf_op jit(solution)/shard_map/all_to_all | solution.py:68
  402.1 7.6 %reshape.112 = bf16[2048,16,16]{2,1,0:T(8,128)(2,1)} reshape(bf16[8,2,32768]{2,1,0:T(2,128)(2,1)S(1)} %all-to-all-done.1) | data formatting | bytes 2097152
  409.7 9.1 %copy.26 = bf16[16,256,8,16]{1,3,2,0:T(8,128)(2,1)} copy(bf16[16,256,8,16]{3,0,1,2:T(8,128)(2,1)} %bitcast.73) | data formatting | bytes 2097152 | tf_op jit(solution)/shard_map/all_to_all | solution.py:68
  (63 shorter events, 12.4 us)
Async XLA Ops:
  7.2 262.2 %copy-start = (bf16[256,2048]{1,0:T(8,128)(2,1)S(1)}, bf16[256,2048]{1,0:T(8,128)(2,1)}, u32[]{:S(2)}) copy-start(bf16[256,2048]{1,0:T(8,128)(2,1)} %param.16) | copy-start | bytes 3145732
  7.2 4.8 %copy-start.14 = (s32[1,2]{1,0:T(1,128)S(1)}, s32[1,2]{1,0:T(1,128)}, u32[]{:S(2)}) copy-start(s32[1,2]{1,0:T(1,128)} %param.13) | copy-start | bytes 28
  7.2 9.8 %copy-start.11 = (bf16[1,2048]{1,0:T(2,128)(2,1)S(1)}, bf16[1,2048]{1,0:T(2,128)(2,1)}, u32[]{:S(2)}) copy-start(bf16[1,2048]{1,0:T(2,128)(2,1)} %param.15) | copy-start | bytes 12292
  7.2 39.0 %all-gather.6.cloned.1.call-start = ((), (), s32[]{:S(2)}) async-start(), calls=%async_computation.4 | async-start | bytes 5242880 | tf_op jit(solution)/shard_map/all_gather | solution.py:44
  10.5 160.0 %all-gather.10.cloned.1.call-start = ((), (), s32[]{:S(2)}) async-start(), calls=%async_computation.6 | async-start | bytes 9437184 | tf_op jit(solution)/shard_map/all_gather | solution.py:35
  11.2 208.0 %all-gather.8.cloned.1.call-start = ((), (), s32[]{:S(2)}) async-start(), calls=%async_computation.5 | async-start | bytes 5242880 | tf_op jit(solution)/shard_map/all_gather | solution.py:44
  186.3 64.7 %all-to-all-start = ((bf16[4,256,2048]{2,1,0:T(8,128)(2,1)}), bf16[4,256,2048]{2,1,0:T(8,128)(2,1)}, u32[]{:S(2)}, u32[]{:S(2)}) async-start(bf16[4,256,2048]{2,1,0:T(8,128)(2,1)} %multiply_convert_fusion.1), calls=%async_computation | async-start | bytes 8388608 | tf_op jit(solution)/shard_map/all_to_all | solution.py:51
  219.2 3.4 copy-start.7
  237.2 18.8 %copy-start.10 = (s32[1,2,2,16,16]{4,3,2,1,0:T(8,128)S(1)}, s32[1,2,2,16,16]{4,3,2,1,0:T(8,128)}, u32[]{:S(2)}) copy-start(s32[1,2,2,16,16]{4,3,2,1,0:T(8,128)} %param.12) | copy-start | bytes 12292
  237.2 19.0 %copy-start.4 = (bf16[1,2,16,16,2048]{4,3,2,1,0:T(8,128)(2,1)S(1)}, bf16[1,2,16,16,2048]{4,3,2,1,0:T(8,128)(2,1)}, u32[]{:S(2)}) copy-start(bf16[1,2,16,16,2048]{4,3,2,1,0:T(8,128)(2,1)} %param.10) | copy-start | bytes 6291460
  237.2 19.6 %copy-start.12 = (bf16[2048]{0:T(1024)(128)(2,1)S(1)}, bf16[2048]{0:T(1024)(128)(2,1)}, u32[]{:S(2)}) copy-start(bf16[2048]{0:T(1024)(128)(2,1)} %param.17) | copy-start | bytes 12292
  251.0 53.1 %all-to-all-start.2 = ((bf16[4,256,2048]{2,1,0:T(8,128)(2,1)}), bf16[4,256,2048]{2,1,0:T(8,128)(2,1)}, u32[]{:S(2)}, u32[]{:S(2)}) async-start(bf16[4,256,2048]{2,1,0:T(8,128)(2,1)} %multiply_convert_fusion), calls=%async_computation.2 | async-start | bytes 8388608 | tf_op jit(solution)/shard_map/all_to_all | solution.py:51
  264.5 4.9 %copy-start.5 = (f32[512,2048]{1,0:T(8,128)}, f32[512,2048]{1,0:T(8,128)S(1)}, u32[]{:S(2)}) copy-start(f32[512,2048]{1,0:T(8,128)S(1)} %bitcast_add_fusion) | copy-start | bytes 12582916
  264.5 4.9 %copy-start.2 = (bf16[1,1,16,16,2048]{4,3,2,1,0:T(8,128)(2,1)S(1)}, bf16[1,1,16,16,2048]{4,3,2,1,0:T(8,128)(2,1)}, u32[]{:S(2)}) copy-start(bf16[1,1,16,16,2048]{4,3,2,1,0:T(8,128)(2,1)} %get-tuple-element.8) | copy-start | bytes 3145732
  271.5 36.0 %copy-start.1 = (bf16[1,1,16,16,2048]{4,3,2,1,0:T(8,128)(2,1)S(1)}, bf16[1,1,16,16,2048]{4,3,2,1,0:T(8,128)(2,1)}, u32[]{:S(2)}) copy-start(bf16[1,1,16,16,2048]{4,3,2,1,0:T(8,128)(2,1)} %get-tuple-element.9) | copy-start | bytes 3145732
  304.1 3.4 copy-start.6
  307.5 1.6 copy-start.3
  309.6 8.8 %copy-start.9 = (bf16[256,2048]{1,0:T(8,128)(2,1)}, bf16[256,2048]{1,0:T(8,128)(2,1)S(1)}, u32[]{:S(2)}) copy-start(bf16[256,2048]{1,0:T(8,128)(2,1)S(1)} %get-tuple-element.15) | copy-start | bytes 3145732
  309.6 33.6 %copy-start.8 = (bf16[256,2048]{1,0:T(8,128)(2,1)}, bf16[256,2048]{1,0:T(8,128)(2,1)S(1)}, u32[]{:S(2)}) copy-start(bf16[256,2048]{1,0:T(8,128)(2,1)S(1)} %get-tuple-element.14) | copy-start | bytes 3145732
  337.1 33.6 %all-to-all-start.3 = ((bf16[8,2,32768]{2,1,0:T(2,128)(2,1)}), bf16[8,2,32768]{2,1,0:T(2,128)(2,1)S(1)}, u32[]{:S(2)}, u32[]{:S(2)}) async-start(bf16[8,2,32768]{2,1,0:T(2,128)(2,1)} %reshape.109), calls=%async_computation.3 | async-start | bytes 2097152 | tf_op jit(solution)/shard_map/all_to_all | solution.py:68
  359.5 17.3 %copy-start.13 = (bf16[1024]{0:T(1024)(128)(2,1)S(1)}, bf16[1024]{0:T(1024)(128)(2,1)}, u32[]{:S(2)}) copy-start(bf16[1024]{0:T(1024)(128)(2,1)} %param.19) | copy-start | bytes 6148
  370.7 31.4 %all-to-all-start.1 = ((bf16[8,2,32768]{2,1,0:T(2,128)(2,1)}), bf16[8,2,32768]{2,1,0:T(2,128)(2,1)S(1)}, u32[]{:S(2)}, u32[]{:S(2)}) async-start(bf16[8,2,32768]{2,1,0:T(2,128)(2,1)} %reshape.111), calls=%async_computation.1 | async-start | bytes 2097152 | tf_op jit(solution)/shard_map/all_to_all | solution.py:68
Sparse Core Ops, SparseCore 0:
  10.6 35.5 all-gather.5
  48.3 122.0 all-gather.9
  172.0 47.1 all-gather.7

commit v2 on v1

--- a/solution.py
+++ b/solution.py
@@ -1,7 +1,18 @@
+import functools
+
 import jax
 import jax.numpy as jnp
 from jax import lax
+from jax.experimental import pallas as pl
+from jax.experimental.pallas import tpu as pltpu
 from jax.sharding import PartitionSpec as P
+
+F32 = jnp.float32
+BF16 = jnp.bfloat16
+BLOCKS = 4
+LINE = 4
+PAIR = 2
+MIB = 1 << 20
 
 
 def rms_norm(inputs, gain):
@@ -71,6 +82,396 @@
     return (learner_rows[None], values[None])
 
 
+def window_kernel(
+    w_ref, own_ref, opp_ref, onehot_ref, picks_ref, gain_ref, table_ref, vgain_ref, up_ref, vout_ref,
+    out_ref, val_ref,
+    wbuf, rows, own_n, joint, to_sib, from_sib, to_x, from_x, picks_all, jrow, jsend, arecv,
+    w_send, w_recv, o_send, o_recv, p_send, p_recv, s_send, s_recv, x_send, x_recv, a_send, a_recv,
+):
+    blocks, env, depth, width = wbuf.shape
+    rounds, count, model = own_ref.shape
+    steps, envs = arecv.shape[1], arecv.shape[3]
+    league_me = lax.axis_index("league")
+    me = lax.axis_index("env")
+    x, core = league_me // 2, league_me % 2
+    z, y = me // PAIR, me % PAIR
+    sib = x * 2 + (1 - core)
+    across = (1 - x) * 2 + core
+    diag = (1 - x) * 2 + (1 - core)
+    y_peer = z * PAIR + (1 - y)
+
+    barrier = pltpu.get_barrier_semaphore()
+    for group in (sib, across, diag):
+        pl.semaphore_signal(barrier, inc=1, device_id=(group, me), device_id_type=pl.DeviceIdType.MESH)
+    for d in range(1, env):
+        pl.semaphore_signal(barrier, inc=1, device_id=(league_me, (me + d) % env), device_id_type=pl.DeviceIdType.MESH)
+    pl.semaphore_wait(barrier, 3 + env - 1)
+
+    def remote(src, dst, send, recv, group, place):
+        return pltpu.make_async_remote_copy(
+            src_ref=src, dst_ref=dst, send_sem=send, recv_sem=recv,
+            device_id=(group, place), device_id_type=pl.DeviceIdType.MESH,
+        )
+
+    def w_copy(b, line, way, place):
+        slot = line * PAIR + y
+        return remote(
+            wbuf.at[b, slot], wbuf.at[b, slot], w_send.at[b, line, way], w_recv.at[b, slot], league_me, place
+        )
+
+    def to_right(b, line):
+        return w_copy(b, line, 0, me + PAIR)
+
+    def to_left(b, line):
+        return w_copy(b, line, 1, me - PAIR)
+
+    def to_y(b, line):
+        return w_copy(b, line, 2, y_peer)
+
+    def w_wait(b, slot):
+        remote(
+            wbuf.at[b, slot], wbuf.at[b, slot], w_send.at[b, 0, 2], w_recv.at[b, slot], league_me, y_peer
+        ).wait_recv()
+
+    def own_sends(b):
+        @pl.when(z < LINE - 1)
+        def _():
+            to_right(b, z).start()
+
+        @pl.when(z > 0)
+        def _():
+            to_left(b, z).start()
+
+        to_y(b, z).start()
+
+    def hops(b):
+        for h in range(1, LINE):
+            low, high = z - h, z + h
+
+            @pl.when(low >= 0)
+            def _():
+                w_wait(b, low * PAIR + y)
+
+                @pl.when(z < LINE - 1)
+                def _():
+                    to_right(b, low).start()
+
+                to_y(b, low).start()
+
+            @pl.when(high < LINE)
+            def _():
+                w_wait(b, high * PAIR + y)
+
+                @pl.when(z > 0)
+                def _():
+                    to_left(b, high).start()
+
+                to_y(b, high).start()
+
+    def finish_w_sends(b):
+        for line in range(LINE):
+            @pl.when(jnp.logical_and(line <= z, z < LINE - 1))
+            def _():
+                to_right(b, line).wait_send()
+
+            @pl.when(jnp.logical_and(line >= z, z > 0))
+            def _():
+                to_left(b, line).wait_send()
+
+            to_y(b, line).wait_send()
+
+    def o_copy(r, way):
+        if way == 0:
+            src, dst, group = opp_ref.at[r], rows.at[league_me, r], across
+        elif way == 1:
+            src, dst, group = opp_ref.at[r], rows.at[league_me, r], sib
+        else:
+            src, dst, group = rows.at[across, r], rows.at[across, r], sib
+        return remote(src, dst, o_send.at[way, r], o_recv.at[way, r], group, me)
+
+    def norm(src, dst, gain, tile=64):
+        def step(i, _):
+            at = pl.ds(pl.multiple_of(i * tile, tile), tile)
+            v = src[at, :].astype(F32)
+            scale = lax.rsqrt(jnp.mean(v * v, axis=-1, keepdims=True) + 1e-05)
+            dst[at, :] = (v * scale * gain[...]).astype(BF16)
+            return 0
+
+        lax.fori_loop(0, count // tile, step, 0)
+
+    for b in range(blocks):
+        wbuf[b, me] = w_ref[:, b * width:(b + 1) * width]
+    own_sends(0)
+    picks_all[league_me] = picks_ref[...]
+    pick_copies = [
+        remote(picks_ref, picks_all.at[league_me], p_send.at[i], p_recv.at[i], group, me)
+        for i, group in enumerate((sib, across, diag))
+    ]
+    for copy in pick_copies:
+        copy.start()
+    for r in range(rounds):
+        o_copy(r, 0).start()
+    for r in range(rounds):
+        o_copy(r, 1).start()
+    own_sends(1)
+    for r in range(rounds):
+        norm(own_ref.at[r], own_n.at[r], gain_ref)
+    hops(0)
+    own_sends(2)
+    for r in range(rounds):
+        norm(opp_ref.at[r], rows.at[league_me, r], gain_ref)
+    for r in range(rounds):
+        o_copy(r, 1).wait_recv()
+        norm(rows.at[sib, r], rows.at[sib, r], gain_ref)
+    hops(1)
+    own_sends(3)
+
+    def base(i, _):
+        b, r = i // rounds, i % rounds
+        cols = pl.ds(pl.multiple_of(b * width, width), width)
+        acts = jnp.dot(onehot_ref[r], table_ref[:, cols], preferred_element_type=F32)
+        joint[b, r] = own_ref[r, :, cols].astype(F32) + opp_ref[r, :, cols].astype(F32) + acts
+        return 0
+
+    lax.fori_loop(0, blocks * rounds, base, 0)
+    for copy in pick_copies:
+        copy.wait_recv()
+    for r in range(rounds):
+        o_copy(r, 0).wait_recv()
+        o_copy(r, 2).start()
+    for r in range(rounds):
+        o_copy(r, 2).wait_recv()
+        norm(rows.at[diag, r], rows.at[diag, r], gain_ref)
+    for r in range(rounds):
+        o_copy(r, 2).wait_send()
+        norm(rows.at[across, r], rows.at[across, r], gain_ref)
+
+    def s_copy(b, k):
+        return remote(to_sib.at[b, k], from_sib.at[b, k], s_send.at[b, k], s_recv.at[b, k], sib, me)
+
+    def x_copy(b):
+        return remote(to_x.at[b], from_x.at[b], x_send.at[b], x_recv.at[b], across, me)
+
+    mine = league_me.astype(F32)
+
+    def each_round(body):
+        def step(r, _):
+            body(r)
+            return 0
+
+        lax.fori_loop(0, rounds, step, 0)
+
+    def block(b, _):
+        @pl.when(b + 2 < blocks)
+        def _():
+            hops(b + 2)
+
+        for line in range(LINE):
+            w_wait(b, line * PAIR + (1 - y))
+
+        def dot(lhs):
+            return jnp.dot(lhs, wbuf[b].reshape(env * depth, width), preferred_element_type=F32)
+
+        def served(group, r):
+            chosen = picks_all[group, pl.ds(r, 1), :][:, :1]
+            return dot(rows[group, r]) * jnp.where(chosen == mine, 1.0, 0.0)
+
+        def first(r):
+            to_sib[b, 0, r] = served(diag, r).astype(BF16)
+
+        each_round(first)
+        s_copy(b, 0).start()
+
+        def second(r):
+            to_sib[b, 1, r] = served(sib, r).astype(BF16)
+
+        each_round(second)
+        s_copy(b, 1).start()
+
+        def third(r):
+            to_x[b, r] = served(across, r).astype(BF16)
+
+        each_round(third)
+        s_copy(b, 0).wait_recv()
+
+        def combine(r):
+            to_x[b, r] = to_x[b, r] + from_sib[b, 0, r]
+
+        each_round(combine)
+        x_copy(b).start()
+
+        def fourth(r):
+            joint[b, r] += dot(own_n[r])
+
+        each_round(fourth)
+
+        def fifth(r):
+            joint[b, r] += served(league_me, r)
+
+        each_round(fifth)
+        s_copy(b, 1).wait_recv()
+
+        def sixth(r):
+            joint[b, r] += from_sib[b, 1, r].astype(F32)
+
+        each_round(sixth)
+        return 0
+
+    lax.fori_loop(0, blocks, block, 0)
+
+    row = lax.broadcasted_iota(jnp.int32, (count, count), 0)
+    col = lax.broadcasted_iota(jnp.int32, (count, count), 1)
+    order = jnp.where(col == (row % envs) * steps + row // envs, 1.0, 0.0).astype(BF16)
+    share = model // env
+
+    def a_copy(r, d):
+        target = (me + d) % env
+        return remote(
+            jsend.at[target, r], arecv.at[r, :, me], a_send.at[r, d], a_recv.at[r, d], league_me, target
+        )
+
+    for b in range(blocks):
+        x_copy(b).wait_recv()
+    tile = 64
+
+    def joint_round(r):
+        def joint_tile(i, _):
+            at = pl.ds(pl.multiple_of(i * tile, tile), tile)
+            parts = [joint[b, r, at, :] + from_x[b, r, at, :].astype(F32) for b in range(blocks)]
+            total = sum(jnp.sum(p * p, axis=-1, keepdims=True) for p in parts)
+            scale = lax.rsqrt(total * (1.0 / model) + 1e-05)
+            for b in range(blocks):
+                cols = slice(b * width, (b + 1) * width)
+                jrow[r, at, cols] = (parts[b] * scale * vgain_ref[:, cols]).astype(BF16)
+            return 0
+
+        lax.fori_loop(0, count // tile, joint_tile, 0)
+        for e in range(env):
+            moved = jnp.dot(order, jrow[r, :, e * share:(e + 1) * share], preferred_element_type=F32)
+            jsend[e, r] = moved.astype(BF16).reshape(steps, envs, share)
+        for d in range(1, env):
+            a_copy(r, d).start()
+
+    for r in range(rounds):
+        joint_round(r)
+    for r in range(rounds):
+        arecv[r, :, me] = jsend[me, r]
+        hidden = jnp.dot(jrow[r], up_ref[...], preferred_element_type=F32)
+        hidden = (hidden / (1.0 + jnp.exp(-hidden))).astype(BF16)
+        val_ref[r] = lax.dot_general(
+            vout_ref[...], hidden, (((1,), (1,)), ((), ())), preferred_element_type=F32
+        )
+    frow = lax.broadcasted_iota(jnp.int32, (share, share), 0)
+    fcol = lax.broadcasted_iota(jnp.int32, (share, share), 1)
+    same = jnp.where(frow == fcol, 1.0, 0.0).astype(BF16)
+    for r in range(rounds):
+        for d in range(1, env):
+            a_copy(r, d).wait_recv()
+
+        def turn(t, _):
+            piece = arecv[r, t].reshape(env * envs, share)
+            out_ref[r, t] = lax.dot_general(
+                same, piece, (((1,), (1,)), ((), ())), preferred_element_type=F32
+            ).astype(BF16)
+            return 0
+
+        lax.fori_loop(0, steps, turn, 0)
+
+    for b in range(blocks):
+        finish_w_sends(b)
+        s_copy(b, 0).wait_send()
+        s_copy(b, 1).wait_send()
+        x_copy(b).wait_send()
+    for copy in pick_copies:
+        copy.wait_send()
+    for r in range(rounds):
+        o_copy(r, 0).wait_send()
+        o_copy(r, 1).wait_send()
+        for d in range(1, env):
+            a_copy(r, d).wait_send()
+
+
+def fused(
+    obs_own,
+    obs_opp,
+    actions,
+    opponent_picks,
+    policy_weight,
+    policy_gain,
+    action_table,
+    value_gain,
+    value_up,
+    value_out,
+):
+    rounds, envs, steps, model = obs_own.shape[1:]
+    count = envs * steps
+    env = lax.axis_size("env")
+    groups = lax.axis_size("league")
+    depth = policy_weight.shape[1]
+    width = model // BLOCKS
+    share = model // env
+    hidden = value_up.shape[1]
+    action_range = jnp.arange(action_table.shape[0], dtype=jnp.int32)
+    ids = actions[0].reshape(2, rounds, count)
+    onehot = (ids[0][:, :, None] == action_range).astype(BF16) + (
+        ids[1][:, :, None] == action_range
+    ).astype(BF16)
+    picks = jnp.zeros((8, 128), F32).at[:rounds].set(opponent_picks[0].astype(F32)[:, None])
+    vmem = pl.BlockSpec(memory_space=pltpu.VMEM)
+    dma = pltpu.SemaphoreType.DMA
+    out, val = pl.pallas_call(
+        window_kernel,
+        out_shape=(
+            jax.ShapeDtypeStruct((rounds, steps, share, env * envs), BF16),
+            jax.ShapeDtypeStruct((rounds, 8, count), F32),
+        ),
+        in_specs=[vmem] * 10,
+        out_specs=(vmem, vmem),
+        scratch_shapes=[
+            pltpu.VMEM((BLOCKS, env, depth, width), BF16),
+            pltpu.VMEM((groups, rounds, count, model), BF16),
+            pltpu.VMEM((rounds, count, model), BF16),
+            pltpu.VMEM((BLOCKS, rounds, count, width), F32),
+            pltpu.VMEM((BLOCKS, 2, rounds, count, width), BF16),
+            pltpu.VMEM((BLOCKS, 2, rounds, count, width), BF16),
+            pltpu.VMEM((BLOCKS, rounds, count, width), BF16),
+            pltpu.VMEM((BLOCKS, rounds, count, width), BF16),
+            pltpu.VMEM((groups, 8, 128), F32),
+            pltpu.VMEM((rounds, count, model), BF16),
+            pltpu.VMEM((env, rounds, steps, envs, share), BF16),
+            pltpu.VMEM((rounds, steps, env, envs, share), BF16),
+            dma((BLOCKS, LINE, 3)),
+            dma((BLOCKS, env)),
+            dma((3, rounds)),
+            dma((3, rounds)),
+            dma((3,)),
+            dma((3,)),
+            dma((BLOCKS, 2)),
+            dma((BLOCKS, 2)),
+            dma((BLOCKS,)),
+            dma((BLOCKS,)),
+            dma((rounds, env)),
+            dma((rounds, env)),
+        ],
+        compiler_params=pltpu.CompilerParams(
+            collective_id=0, has_side_effects=True, vmem_limit_bytes=62 * MIB
+        ),
+    )(
+        policy_weight[0],
+        obs_own[0].reshape(rounds, count, model),
+        obs_opp[0].reshape(rounds, count, model),
+        onehot,
+        picks,
+        policy_gain.astype(F32),
+        action_table,
+        value_gain.astype(F32)[None],
+        value_up,
+        jnp.broadcast_to(value_out[None], (8, hidden)),
+    )
+    values = val[:, 0].reshape(1, rounds, envs, steps)
+    return (out[None], values)
+
+
 def solution(mesh):
     in_specs = (
         P("league", None, "env", None, None),
@@ -85,4 +486,5 @@
         P(),
     )
     out_specs = (P("league", None, None, "env", None), P("league", None, "env", None))
-    return jax.shard_map(local, mesh=mesh, in_specs=in_specs, out_specs=out_specs, check_vma=False)
+    body = fused if mesh.shape["env"] == LINE * PAIR else local
+    return jax.shard_map(body, mesh=mesh, in_specs=in_specs, out_specs=out_specs, check_vma=False)

time: 432 us -> 186 us (0.43)
  waiting for transfers between devices: 226 us -> 0 us
  Pallas kernels: 0 us -> 174 us
  local copies, waits for them, and re-layouts: 95.6 us -> 7.42 us
  matrix products: 41.7 us -> 0 us
  starting transfers between devices: 22.1 us -> 0 us
  other arithmetic: 24.9 us -> 4.15 us
  between operations: 14 us -> 0.64 us
  blocking collectives: 5.04 us -> 0 us
    all_gather x3 -> x0, waiting for transfers between devices: 178 us -> none  [the longest x1 121 us: local(): own_whole = lax.all_gather(weight_shard, 'env', axis=0, tiled=True)]
    pallas_call x0 -> x1, Pallas kernels: none -> 174 us  [fused(): pl.pallas_call(window_kernel, out_shape=(jax.ShapeDtypeStruct((rounds, st...]
    unnamed x38 -> x1, local copies, waits for them, and re-layouts: 56 us -> 3.13 us
    all_to_all x4 -> x0, waiting for transfers between devices: 46.4 us -> none  [the longest x2 46.4 us: local(): lax.all_to_all(products, 'league', split_axis=0, concat_axis=0, tiled=True)]
    dot_general x7 -> x0, matrix products: 41.7 us -> none  [the longest x2 23.9 us: local(): jnp.dot(all_normed, own_whole, preferred_element_type=jnp.float32)]
    all_to_all x4 -> x0, starting transfers between devices: 22 us -> none  [the longest x2 12 us: local(): lax.all_to_all(time_block, 'env', split_axis=1, concat_axis=2, tiled=True)]
    all_to_all x2 -> x0, local copies, waits for them, and re-layouts: 18.2 us -> none  [local(): lax.all_to_all(time_block, 'env', split_axis=1, concat_axis=2, tiled=True)]
    reshape x2 -> x0, local copies, waits for them, and re-layouts: 17.6 us -> none  [local(): joint_row.reshape(env_count, step_count, model_width).transpose(1, 2, 0)]
  transfers between devices with their start and end apart: 7 -> 0, of which waited for: 5 -> 0; matrix products, arithmetic and copies ran while one was open for 24% -> 0% of each run, Pallas kernels for 0% -> 0%
where the time goes in v2:
time: 186 us
  Pallas kernels  174 us (94%)
  local copies, waits for them, and re-layouts  7.42 us (4%)
  other arithmetic  4.15 us (2%)
    pallas_call x1, Pallas kernels, fused(): pl.pallas_call(window_kernel, out_shape=(jax.ShapeDtypeStruct((rounds, st...  174 us

profile of v2, /device:TPU:12, one launch (start us, length us, event | category | flops | bytes accessed | tf_op | source)
XLA Modules:
  0.0 185.8 jit_solution(17346475260373492991)
XLA Ops:
  0.6 0.7 convert_bitcast_fusion
  1.3 0.7 scatter.8.picks_ref
  2.0 1.3 convert_element_type.24.gain_ref
  3.3 1.3 broadcast_in_dim.12
  4.5 1.3 broadcast_in_dim.10.vout_ref
  5.8 0.7 fusion.3
  6.6 0.1 eq.30
  6.6 0.1 eq.34
  6.7 0.9 fusion.2.onehot_ref
  7.6 173.6 %shard_map.113 = (bf16[2,16,256,128]{3,2,1,0:T(8,128)(2,1)}, f32[2,8,256]{2,1,0:T(8,128)}) custom-call(bf16[256,2048]{1,0:T(8,128)(2,1)} %bitcast.14, bf16[2,256,2048]{2,1,0:T(8,128)(2,1)} %bitcast.11, bf16[2,256,2048]{2,1,0:T(8,128)(2,1)} %bitcast.12, bf16[2,256,256]{2,1,0:T(8,128)(2,1)} %fusion.2.onehot_ref, f32[8,128]{1,0:T(8,128)} %scatter.8.picks_ref, ...), custom_call_target="tpu_custom_call" | custom-call | tf_op jit(solution)/shard_map/pallas_call | solution.py:422
  181.2 0.7 slice_reduce_fusion
  181.9 0.7 reshape_squeeze.12
  182.6 3.1 %copy.13 = bf16[1,2,16,256,128]{4,3,2,1,0:T(8,128)(2,1)} copy(bf16[1,2,16,256,128]{4,3,2,1,0:T(8,128)(2,1)} %bitcast.13) | data formatting | bytes 4194304
  (1 shorter events, 0.0 us)

commit v3 on v2

--- a/solution.py
+++ b/solution.py
@@ -83,7 +83,7 @@
 
 
 def window_kernel(
-    w_ref, own_ref, opp_ref, onehot_ref, picks_ref, gain_ref, table_ref, vgain_ref, up_ref, vout_ref,
+    w_ref, own_ref, opp_ref, onehot_ref, small_ref, table_ref, up_ref,
     out_ref, val_ref,
     wbuf, rows, own_n, joint, to_sib, from_sib, to_x, from_x, picks_all, jrow, jsend, arecv,
     w_send, w_recv, o_send, o_recv, p_send, p_recv, s_send, s_recv, x_send, x_recv, a_send, a_recv,
@@ -144,29 +144,32 @@
 
         to_y(b, z).start()
 
+    def hop(b, h):
+        low, high = z - h, z + h
+
+        @pl.when(low >= 0)
+        def _():
+            w_wait(b, low * PAIR + y)
+
+            @pl.when(z < LINE - 1)
+            def _():
+                to_right(b, low).start()
+
+            to_y(b, low).start()
+
+        @pl.when(high < LINE)
+        def _():
+            w_wait(b, high * PAIR + y)
+
+            @pl.when(z > 0)
+            def _():
+                to_left(b, high).start()
+
+            to_y(b, high).start()
+
     def hops(b):
         for h in range(1, LINE):
-            low, high = z - h, z + h
-
-            @pl.when(low >= 0)
-            def _():
-                w_wait(b, low * PAIR + y)
-
-                @pl.when(z < LINE - 1)
-                def _():
-                    to_right(b, low).start()
-
-                to_y(b, low).start()
-
-            @pl.when(high < LINE)
-            def _():
-                w_wait(b, high * PAIR + y)
-
-                @pl.when(z > 0)
-                def _():
-                    to_left(b, high).start()
-
-                to_y(b, high).start()
+            hop(b, h)
 
     def finish_w_sends(b):
         for line in range(LINE):
@@ -194,17 +197,19 @@
             at = pl.ds(pl.multiple_of(i * tile, tile), tile)
             v = src[at, :].astype(F32)
             scale = lax.rsqrt(jnp.mean(v * v, axis=-1, keepdims=True) + 1e-05)
-            dst[at, :] = (v * scale * gain[...]).astype(BF16)
+            dst[at, :] = (v * scale * gain).astype(BF16)
             return 0
 
         lax.fori_loop(0, count // tile, step, 0)
 
+    gain = small_ref[0:1, :]
+    tag = small_ref.at[:, 0:128]
     for b in range(blocks):
         wbuf[b, me] = w_ref[:, b * width:(b + 1) * width]
     own_sends(0)
-    picks_all[league_me] = picks_ref[...]
+    picks_all[league_me] = tag[...]
     pick_copies = [
-        remote(picks_ref, picks_all.at[league_me], p_send.at[i], p_recv.at[i], group, me)
+        remote(tag, picks_all.at[league_me], p_send.at[i], p_recv.at[i], group, me)
         for i, group in enumerate((sib, across, diag))
     ]
     for copy in pick_copies:
@@ -215,16 +220,16 @@
         o_copy(r, 1).start()
     own_sends(1)
     for r in range(rounds):
-        norm(own_ref.at[r], own_n.at[r], gain_ref)
+        norm(own_ref.at[r], own_n.at[r], gain)
     hops(0)
     own_sends(2)
     for r in range(rounds):
-        norm(opp_ref.at[r], rows.at[league_me, r], gain_ref)
-    for r in range(rounds):
-        o_copy(r, 1).wait_recv()
-        norm(rows.at[sib, r], rows.at[sib, r], gain_ref)
+        norm(opp_ref.at[r], rows.at[league_me, r], gain)
     hops(1)
     own_sends(3)
+    for r in range(rounds):
+        o_copy(r, 1).wait_recv()
+        norm(rows.at[sib, r], rows.at[sib, r], gain)
 
     def base(i, _):
         b, r = i // rounds, i % rounds
@@ -236,88 +241,56 @@
     lax.fori_loop(0, blocks * rounds, base, 0)
     for copy in pick_copies:
         copy.wait_recv()
-    for r in range(rounds):
-        o_copy(r, 0).wait_recv()
-        o_copy(r, 2).start()
-    for r in range(rounds):
-        o_copy(r, 2).wait_recv()
-        norm(rows.at[diag, r], rows.at[diag, r], gain_ref)
-    for r in range(rounds):
-        o_copy(r, 2).wait_send()
-        norm(rows.at[across, r], rows.at[across, r], gain_ref)
-
-    def s_copy(b, k):
-        return remote(to_sib.at[b, k], from_sib.at[b, k], s_send.at[b, k], s_recv.at[b, k], sib, me)
-
-    def x_copy(b):
-        return remote(to_x.at[b], from_x.at[b], x_send.at[b], x_recv.at[b], across, me)
+
+    def s_copy(b, r, k):
+        return remote(to_sib.at[b, k, r], from_sib.at[b, k, r], s_send.at[b, r, k], s_recv.at[b, r, k], sib, me)
+
+    def x_copy(b, r):
+        return remote(to_x.at[b, r], from_x.at[b, r], x_send.at[b, r], x_recv.at[b, r], across, me)
 
     mine = league_me.astype(F32)
 
-    def each_round(body):
-        def step(r, _):
-            body(r)
-            return 0
-
-        lax.fori_loop(0, rounds, step, 0)
-
-    def block(b, _):
-        @pl.when(b + 2 < blocks)
-        def _():
-            hops(b + 2)
-
-        for line in range(LINE):
-            w_wait(b, line * PAIR + (1 - y))
+    def unit(i, _):
+        b, r = i // rounds, i % rounds
+
+        @pl.when(i < (blocks - 2) * (LINE - 1))
+        def _():
+            hop(2 + i // (LINE - 1), i % (LINE - 1) + 1)
+
+        @pl.when(i < rounds)
+        def _():
+            o_copy(r, 0).wait_recv()
+            o_copy(r, 2).start()
+            o_copy(r, 2).wait_recv()
+            norm(rows.at[diag, r], rows.at[diag, r], gain)
+            o_copy(r, 2).wait_send()
+            norm(rows.at[across, r], rows.at[across, r], gain)
+
+        @pl.when(r == 0)
+        def _():
+            for line in range(LINE):
+                w_wait(b, line * PAIR + (1 - y))
 
         def dot(lhs):
             return jnp.dot(lhs, wbuf[b].reshape(env * depth, width), preferred_element_type=F32)
 
-        def served(group, r):
-            chosen = picks_all[group, pl.ds(r, 1), :][:, :1]
+        def served(group):
+            chosen = jnp.where(r == 0, picks_all[group, 3:4, :], picks_all[group, 4:5, :])[:, :1]
             return dot(rows[group, r]) * jnp.where(chosen == mine, 1.0, 0.0)
 
-        def first(r):
-            to_sib[b, 0, r] = served(diag, r).astype(BF16)
-
-        each_round(first)
-        s_copy(b, 0).start()
-
-        def second(r):
-            to_sib[b, 1, r] = served(sib, r).astype(BF16)
-
-        each_round(second)
-        s_copy(b, 1).start()
-
-        def third(r):
-            to_x[b, r] = served(across, r).astype(BF16)
-
-        each_round(third)
-        s_copy(b, 0).wait_recv()
-
-        def combine(r):
-            to_x[b, r] = to_x[b, r] + from_sib[b, 0, r]
-
-        each_round(combine)
-        x_copy(b).start()
-
-        def fourth(r):
-            joint[b, r] += dot(own_n[r])
-
-        each_round(fourth)
-
-        def fifth(r):
-            joint[b, r] += served(league_me, r)
-
-        each_round(fifth)
-        s_copy(b, 1).wait_recv()
-
-        def sixth(r):
-            joint[b, r] += from_sib[b, 1, r].astype(F32)
-
-        each_round(sixth)
+        to_sib[b, 0, r] = served(diag).astype(BF16)
+        s_copy(b, r, 0).start()
+        to_sib[b, 1, r] = served(sib).astype(BF16)
+        s_copy(b, r, 1).start()
+        to_x[b, r] = served(across).astype(BF16)
+        s_copy(b, r, 0).wait_recv()
+        to_x[b, r] = to_x[b, r] + from_sib[b, 0, r]
+        x_copy(b, r).start()
+        joint[b, r] += dot(own_n[r])
+        joint[b, r] += served(league_me)
         return 0
 
-    lax.fori_loop(0, blocks, block, 0)
+    lax.fori_loop(0, blocks * rounds, unit, 0)
 
     row = lax.broadcasted_iota(jnp.int32, (count, count), 0)
     col = lax.broadcasted_iota(jnp.int32, (count, count), 1)
@@ -330,19 +303,24 @@
             jsend.at[target, r], arecv.at[r, :, me], a_send.at[r, d], a_recv.at[r, d], league_me, target
         )
 
-    for b in range(blocks):
-        x_copy(b).wait_recv()
     tile = 64
 
     def joint_round(r):
+        for b in range(blocks):
+            s_copy(b, r, 1).wait_recv()
+            x_copy(b, r).wait_recv()
+
         def joint_tile(i, _):
             at = pl.ds(pl.multiple_of(i * tile, tile), tile)
-            parts = [joint[b, r, at, :] + from_x[b, r, at, :].astype(F32) for b in range(blocks)]
+            parts = [
+                joint[b, r, at, :] + from_sib[b, 1, r, at, :].astype(F32) + from_x[b, r, at, :].astype(F32)
+                for b in range(blocks)
+            ]
             total = sum(jnp.sum(p * p, axis=-1, keepdims=True) for p in parts)
             scale = lax.rsqrt(total * (1.0 / model) + 1e-05)
             for b in range(blocks):
                 cols = slice(b * width, (b + 1) * width)
-                jrow[r, at, cols] = (parts[b] * scale * vgain_ref[:, cols]).astype(BF16)
+                jrow[r, at, cols] = (parts[b] * scale * small_ref[1:2, cols]).astype(BF16)
             return 0
 
         lax.fori_loop(0, count // tile, joint_tile, 0)
@@ -358,9 +336,10 @@
         arecv[r, :, me] = jsend[me, r]
         hidden = jnp.dot(jrow[r], up_ref[...], preferred_element_type=F32)
         hidden = (hidden / (1.0 + jnp.exp(-hidden))).astype(BF16)
+        out_row = jnp.broadcast_to(small_ref[2:3, :up_ref.shape[1]], (8, up_ref.shape[1])).astype(BF16)
         val_ref[r] = lax.dot_general(
-            vout_ref[...], hidden, (((1,), (1,)), ((), ())), preferred_element_type=F32
-        )
+            out_row, hidden, (((1,), (1,)), ((), ())), preferred_element_type=F32
+        )[0:1]
     frow = lax.broadcasted_iota(jnp.int32, (share, share), 0)
     fcol = lax.broadcasted_iota(jnp.int32, (share, share), 1)
     same = jnp.where(frow == fcol, 1.0, 0.0).astype(BF16)
@@ -379,9 +358,10 @@
 
     for b in range(blocks):
         finish_w_sends(b)
-        s_copy(b, 0).wait_send()
-        s_copy(b, 1).wait_send()
-        x_copy(b).wait_send()
+        for r in range(rounds):
+            s_copy(b, r, 0).wait_send()
+            s_copy(b, r, 1).wait_send()
+            x_copy(b, r).wait_send()
     for copy in pick_copies:
         copy.wait_send()
     for r in range(rounds):
@@ -416,16 +396,24 @@
     onehot = (ids[0][:, :, None] == action_range).astype(BF16) + (
         ids[1][:, :, None] == action_range
     ).astype(BF16)
-    picks = jnp.zeros((8, 128), F32).at[:rounds].set(opponent_picks[0].astype(F32)[:, None])
+    small = jnp.concatenate(
+        [
+            policy_gain.astype(F32),
+            value_gain.astype(F32)[None],
+            jnp.pad(value_out.astype(F32), (0, model - hidden))[None],
+            jnp.broadcast_to(opponent_picks[0].astype(F32)[:, None], (rounds, model)),
+            jnp.zeros((5 - rounds, model), F32),
+        ]
+    )
     vmem = pl.BlockSpec(memory_space=pltpu.VMEM)
     dma = pltpu.SemaphoreType.DMA
     out, val = pl.pallas_call(
         window_kernel,
         out_shape=(
             jax.ShapeDtypeStruct((rounds, steps, share, env * envs), BF16),
-            jax.ShapeDtypeStruct((rounds, 8, count), F32),
+            jax.ShapeDtypeStruct((rounds, 1, count), F32),
         ),
-        in_specs=[vmem] * 10,
+        in_specs=[vmem] * 7,
         out_specs=(vmem, vmem),
         scratch_shapes=[
             pltpu.VMEM((BLOCKS, env, depth, width), BF16),
@@ -446,10 +434,10 @@
             dma((3, rounds)),
             dma((3,)),
             dma((3,)),
-            dma((BLOCKS, 2)),
-            dma((BLOCKS, 2)),
-            dma((BLOCKS,)),
-            dma((BLOCKS,)),
+            dma((BLOCKS, rounds, 2)),
+            dma((BLOCKS, rounds, 2)),
+            dma((BLOCKS, rounds)),
+            dma((BLOCKS, rounds)),
             dma((rounds, env)),
             dma((rounds, env)),
         ],
@@ -461,14 +449,11 @@
         obs_own[0].reshape(rounds, count, model),
         obs_opp[0].reshape(rounds, count, model),
         onehot,
-        picks,
-        policy_gain.astype(F32),
+        small,
         action_table,
-        value_gain.astype(F32)[None],
         value_up,
-        jnp.broadcast_to(value_out[None], (8, hidden)),
     )
-    values = val[:, 0].reshape(1, rounds, envs, steps)
+    values = val.reshape(1, rounds, envs, steps)
     return (out[None], values)
 
 

time: 186 us -> 173 us (0.930)
  Pallas kernels: 174 us -> 162 us
    pallas_call x1, Pallas kernels: 174 us -> 162 us  [fused(): pl.pallas_call(window_kernel, out_shape=(jax.ShapeDtypeStruct((rounds, st...]
where the time goes in v3:
time: 173 us
  Pallas kernels  162 us (94%)
  local copies, waits for them, and re-layouts  6.17 us (4%)
  other arithmetic  3.63 us (2%)
    pallas_call x1, Pallas kernels, fused(): pl.pallas_call(window_kernel, out_shape=(jax.ShapeDtypeStruct((rounds, st...  162 us

profile of v3, /device:TPU:12, one launch (start us, length us, event | category | flops | bytes accessed | tf_op | source)
XLA Modules:
  0.0 172.7 jit_solution(9633127366319496113)
XLA Ops:
  0.6 0.7 convert_bitcast_fusion
  1.3 0.7 broadcast_in_dim.33
  2.0 0.7 pad_convert_fusion
  2.7 0.1 broadcast_in_dim.30
  2.7 1.4 concatenate.3.small_ref
  4.1 0.7 fusion.3
  4.9 0.1 eq.30
  4.9 0.1 eq.34
  5.0 0.9 fusion.2.onehot_ref
  5.9 162.2 %shard_map.113 = (bf16[2,16,256,128]{3,2,1,0:T(8,128)(2,1)}, f32[2,1,256]{2,1,0:T(1,128)}) custom-call(bf16[256,2048]{1,0:T(8,128)(2,1)} %bitcast.15, bf16[2,256,2048]{2,1,0:T(8,128)(2,1)} %bitcast.13, bf16[2,256,2048]{2,1,0:T(8,128)(2,1)} %bitcast.14, bf16[2,256,256]{2,1,0:T(8,128)(2,1)} %fusion.2.onehot_ref, f32[8,2048]{1,0:T(8,128)} %concatenate.3.small_ref, ...), custom_call_target="tpu_custom_call" | custom-call | tf_op jit(solution)/shard_map/pallas_call | solution.py:410
  168.2 0.7 reduce
  168.9 0.7 reshape.19
  169.6 3.1 %copy.13 = bf16[1,2,16,256,128]{4,3,2,1,0:T(8,128)(2,1)} copy(bf16[1,2,16,256,128]{4,3,2,1,0:T(8,128)(2,1)} %bitcast.12) | data formatting | bytes 4194304
  (1 shorter events, 0.0 us)

commit v4 on v3

--- a/solution.py
+++ b/solution.py
@@ -238,6 +238,7 @@
         joint[b, r] = own_ref[r, :, cols].astype(F32) + opp_ref[r, :, cols].astype(F32) + acts
         return 0
 
+    hops(2)
     lax.fori_loop(0, blocks * rounds, base, 0)
     for copy in pick_copies:
         copy.wait_recv()
@@ -251,13 +252,15 @@
     mine = league_me.astype(F32)
 
     def unit(i, _):
-        b, r = i // rounds, i % rounds
-
-        @pl.when(i < (blocks - 2) * (LINE - 1))
-        def _():
-            hop(2 + i // (LINE - 1), i % (LINE - 1) + 1)
-
-        @pl.when(i < rounds)
+        late = i // (2 * rounds)
+        b = (1 - late) * (i % 2) + late * (i // rounds)
+        r = (1 - late) * (i // 2) + late * (i % rounds)
+
+        @pl.when(i < LINE - 1)
+        def _():
+            hop(3, i + 1)
+
+        @pl.when(jnp.logical_and(i < 2 * rounds, b == 0))
         def _():
             o_copy(r, 0).wait_recv()
             o_copy(r, 2).start()

time: 173 us -> 173 us (level)
  no operation moved by 1% of the time
where the time goes in v4:
time: 173 us
  Pallas kernels  162 us (94%)
  local copies, waits for them, and re-layouts  6.17 us (4%)
  other arithmetic  3.63 us (2%)
    pallas_call x1, Pallas kernels, fused(): pl.pallas_call(window_kernel, out_shape=(jax.ShapeDtypeStruct((rounds, st...  162 us

profile of v4, /device:TPU:12, one launch (start us, length us, event | category | flops | bytes accessed | tf_op | source)
XLA Modules:
  0.0 172.7 jit_solution(758149637810210511)
XLA Ops:
  0.6 0.7 convert_bitcast_fusion
  1.3 0.7 broadcast_in_dim.33
  2.0 0.7 pad_convert_fusion
  2.7 0.1 broadcast_in_dim.30
  2.7 1.4 concatenate.3.small_ref
  4.1 0.7 fusion.3
  4.9 0.1 eq.30
  4.9 0.1 eq.34
  5.0 0.9 fusion.2.onehot_ref
  5.9 162.2 %shard_map.113 = (bf16[2,16,256,128]{3,2,1,0:T(8,128)(2,1)}, f32[2,1,256]{2,1,0:T(1,128)}) custom-call(bf16[256,2048]{1,0:T(8,128)(2,1)} %bitcast.15, bf16[2,256,2048]{2,1,0:T(8,128)(2,1)} %bitcast.13, bf16[2,256,2048]{2,1,0:T(8,128)(2,1)} %bitcast.14, bf16[2,256,256]{2,1,0:T(8,128)(2,1)} %fusion.2.onehot_ref, f32[8,2048]{1,0:T(8,128)} %concatenate.3.small_ref, ...), custom_call_target="tpu_custom_call" | custom-call | tf_op jit(solution)/shard_map/pallas_call | solution.py:413
  168.2 0.7 reduce
  168.9 0.7 reshape.19
  169.6 3.1 %copy.13 = bf16[1,2,16,256,128]{4,3,2,1,0:T(8,128)(2,1)} copy(bf16[1,2,16,256,128]{4,3,2,1,0:T(8,128)(2,1)} %bitcast.12) | data formatting | bytes 4194304
  (1 shorter events, 0.0 us)
